TPU v7x, 32 devices: a whole 2x2x4 slice. The times are simulated.
32 devices in a mesh: fsdp: 8 (over y, x, core), tp: 4 (over z).
Axes of the slice: x: 2, y: 2, z: 4, core: 2. Of those that a mesh axis runs over, the one named last changes fastest.
Arguments:
- tokens: bfloat16 [8192, 2048], P(('fsdp', 'tp')), may hold values from -6 to 6
- norm1_gain: float32 [2048], replicated, may hold values from 0.25 to 1.75
- norm1_shift: float32 [2048], replicated, may hold values from -1 to 1
- w_query: bfloat16 [2048, 2048], P('fsdp', 'tp'), may hold values from -0.125 to 0.125
- b_query: float32 [2048], P('tp'), may hold values from -1 to 1
- w_key: bfloat16 [2048, 2048], P('fsdp', 'tp'), may hold values from -0.125 to 0.125
- w_value: bfloat16 [2048, 2048], P('fsdp', 'tp'), may hold values from -0.125 to 0.125
- b_value: float32 [2048], P('tp'), may hold values from -1 to 1
- w_out: bfloat16 [2048, 2048], P('fsdp', 'tp'), may hold values from -0.5 to 0.5
- b_out: float32 [2048], replicated, may hold values from -1 to 1
- norm2_gain: float32 [2048], replicated, may hold values from 0.25 to 1.75
- norm2_shift: float32 [2048], replicated, may hold values from -1 to 1
- w_up: bfloat16 [2048, 8192], P('fsdp', 'tp'), may hold values from -0.125 to 0.125
- b_up: float32 [8192], P('tp'), may hold values from -1 to 1
- w_down: bfloat16 [2048, 8192], P('fsdp', 'tp'), may hold values from -0.09375 to 0.09375
- b_down: float32 [2048], replicated, may hold values from -1 to 1
- teacher: bfloat16 [8192, 2048], P(('fsdp', 'tp')), may hold values from -6 to 6
- valid_mask: int32 [8192], P(('fsdp', 'tp')), may hold values from 0 to 1, as said below
- parents: int32 [8, 8], P('fsdp'), may hold values from -1 to 6, as said below
- summary: int32 [8, 8, 12], P('fsdp'), may hold values from 0 to 127, as said below
Outputs:
- output_states: bfloat16 [8192, 2048], P(('fsdp', 'tp'))
- mean_loss: float32 [], replicated
- grad_tokens: float32 [8192, 2048], P(('fsdp', 'tp'))
- grad_norm1_gain: float32 [2048], replicated
- grad_norm1_shift: float32 [2048], replicated
- grad_w_query: float32 [2048, 2048], P('fsdp', 'tp')
- grad_b_query: float32 [2048], P('tp')
- grad_w_key: float32 [2048, 2048], P('fsdp', 'tp')
- grad_w_value: float32 [2048, 2048], P('fsdp', 'tp')
- grad_b_value: float32 [2048], P('tp')
- grad_w_out: float32 [2048, 2048], P('fsdp', 'tp')
- grad_b_out: float32 [2048], replicated
- grad_norm2_gain: float32 [2048], replicated
- grad_norm2_shift: float32 [2048], replicated
- grad_w_up: float32 [2048, 8192], P('fsdp', 'tp')
- grad_b_up: float32 [8192], P('tp')
- grad_w_down: float32 [2048, 8192], P('fsdp', 'tp')
- grad_b_down: float32 [2048], replicated
Inputs may be any that keep to these rules, and one draw needn't show every extreme that they name: valid_mask is 1 at the first token of every tree. parents[f, 0] is -1 and 0 <= parents[f, s] < s for every later segment s; the last segment of every tree has the segment before it as parent. `summary`: the 12 offsets of one segment are distinct.
All inputs are finite; a program needn't handle non-finite values.
Results may differ from a plain program's by a relative error of at most 0.019.
Values may be sent and summed in bfloat16 or wider, within the bound.
No kernel may reach another device: no remote copies, remote signals or barrier semaphores. Data moves between devices by JAX's collectives and lax.ppermute only.
A program may use at most 192 MiB of HBM per device.

v0:
```python
import jax
import jax.numpy as jnp
from jax import lax
from jax.sharding import PartitionSpec as P

HD = 64
EPSILON = 1e-05
MASKED_SCORE = -1e30


def layer_norm(vectors, norm_gain, norm_shift):
    centre = jnp.mean(vectors, axis=-1, keepdims=True)
    centred = vectors - centre
    spread = jnp.mean(centred * centred, axis=-1, keepdims=True)
    return centred * lax.rsqrt(spread + EPSILON) * norm_gain + norm_shift


def ancestors(parent_row):
    segments = parent_row.shape[0]
    columns = jnp.arange(segments, dtype=jnp.int32)

    def follow(sweep, state_pair):
        ancestry, current = state_pair
        matches = current[:, None] == columns[None, :]
        ancestry = jnp.maximum(ancestry, matches.astype(jnp.float32))
        following = jnp.sum(jnp.where(matches, parent_row[None, :], 0), axis=1)
        current = jnp.where(current >= 0, following, -1)
        return (ancestry, current)

    start_table = jnp.zeros((segments, segments), jnp.float32)
    ancestry, finished = lax.fori_loop(0, segments, follow, (start_table, parent_row))
    return ancestry


def tree_tables(parent_row, summary_rows, length):
    segments = parent_row.shape[0]
    seg_length = length // segments
    ancestry = ancestors(parent_row)
    offsets = jnp.arange(seg_length, dtype=jnp.int32)
    marked = jnp.max(
        (summary_rows[:, :, None] == offsets[None, None, :]).astype(jnp.float32), axis=1
    ).reshape(length)
    key_segment = jnp.arange(length, dtype=jnp.int32) // seg_length
    key_onehot = (key_segment[:, None] == jnp.arange(segments, dtype=jnp.int32)[None, :]).astype(
        jnp.float32
    )
    return (ancestry, marked, key_segment, key_onehot, seg_length)


def block_mask(tables, start_row, block_rows):
    ancestry, marked, key_segment, key_onehot, seg_length = tables
    query_position = start_row + jnp.arange(block_rows, dtype=jnp.int32)
    query_segment = query_position // seg_length
    query_onehot = (
        query_segment[:, None] == jnp.arange(ancestry.shape[0], dtype=jnp.int32)[None, :]
    ).astype(jnp.float32)
    reached = jnp.dot(jnp.dot(query_onehot, ancestry, precision=None), key_onehot.T, precision=None)
    key_position = jnp.arange(marked.shape[0], dtype=jnp.int32)
    same_segment = (query_segment[:, None] == key_segment[None, :]) & (
        key_position[None, :] <= query_position[:, None]
    )
    return same_segment | (reached > 0.5) & (marked[None, :] > 0.5)


def contract(left_side, right_side, left_dim, right_dim):
    return lax.dot_general(
        left_side,
        right_side,
        (((left_dim,), (right_dim,)), ((), ())),
        preferred_element_type=jnp.float32,
    )


def attend_forward(queries, key_states, value_states, tables):
    length = queries.shape[0]
    head_count = queries.shape[1] // HD
    block_rows = min(512, length)
    query_heads = queries.reshape(length, head_count, HD)
    key_heads = key_states.reshape(length, head_count, HD)
    value_heads = value_states.reshape(length, head_count, HD)

    def one_block(start_row):
        query_block = lax.dynamic_slice_in_dim(query_heads, start_row, block_rows, 0)
        scores = jnp.einsum(
            "qhd,khd->hqk", query_block, key_heads, preferred_element_type=jnp.float32
        )
        allowed = block_mask(tables, start_row, block_rows)
        scores = jnp.where(allowed[None], scores, MASKED_SCORE)
        highest = jnp.max(scores, axis=-1, keepdims=True)
        exp_scores = jnp.exp(scores - highest)
        totals = jnp.sum(exp_scores, axis=-1, keepdims=True)
        shares = (exp_scores / totals).astype(jnp.bfloat16)
        attended = jnp.einsum(
            "hqk,khd->qhd", shares, value_heads, preferred_element_type=jnp.float32
        )
        return (attended.astype(jnp.bfloat16), (highest + jnp.log(totals))[..., 0])

    starts = jnp.arange(length // block_rows, dtype=jnp.int32) * block_rows
    attended, log_totals = lax.map(one_block, starts)
    return (attended.reshape(length, head_count * HD), log_totals)


def attend_backward(queries, key_states, value_states, grad_attended, log_totals, tables):
    length = queries.shape[0]
    head_count = queries.shape[1] // HD
    block_rows = min(512, length)
    query_heads = queries.reshape(length, head_count, HD)
    key_heads = key_states.reshape(length, head_count, HD)
    value_heads = value_states.reshape(length, head_count, HD)
    grad_heads = grad_attended.reshape(length, head_count, HD)

    def one_block(summed, members):
        start_row, log_block = members
        key_sum, value_sum = summed
        query_block = lax.dynamic_slice_in_dim(query_heads, start_row, block_rows, 0)
        grad_block = lax.dynamic_slice_in_dim(grad_heads, start_row, block_rows, 0)
        scores = jnp.einsum(
            "qhd,khd->hqk", query_block, key_heads, preferred_element_type=jnp.float32
        )
        allowed = block_mask(tables, start_row, block_rows)
        probs = jnp.where(allowed[None], jnp.exp(scores - log_block[..., None]), 0.0)
        grad_probs = jnp.einsum(
            "qhd,khd->hqk", grad_block, value_heads, preferred_element_type=jnp.float32
        )
        inner_sum = jnp.sum(probs * grad_probs, axis=-1, keepdims=True)
        grad_scores = (probs * (grad_probs - inner_sum)).astype(jnp.bfloat16)
        grad_query = jnp.einsum(
            "hqk,khd->qhd", grad_scores, key_heads, preferred_element_type=jnp.float32
        ).astype(jnp.bfloat16)
        key_sum = key_sum + jnp.einsum(
            "hqk,qhd->khd", grad_scores, query_block, preferred_element_type=jnp.float32
        )
        value_sum = value_sum + jnp.einsum(
            "hqk,qhd->khd",
            probs.astype(jnp.bfloat16),
            grad_block,
            preferred_element_type=jnp.float32,
        )
        return ((key_sum, value_sum), grad_query)

    starts = jnp.arange(length // block_rows, dtype=jnp.int32) * block_rows
    zero_heads = jnp.zeros((length, head_count, HD), jnp.float32)
    (key_sum, value_sum), grad_queries = lax.scan(
        one_block, (zero_heads, zero_heads), (starts, log_totals)
    )
    width = head_count * HD
    return (
        grad_queries.reshape(length, width),
        key_sum.reshape(length, width).astype(jnp.bfloat16),
        value_sum.reshape(length, width).astype(jnp.bfloat16),
    )


def body(
    tokens,
    norm1_gain,
    norm1_shift,
    w_query,
    b_query,
    w_key,
    w_value,
    b_value,
    w_out,
    b_out,
    norm2_gain,
    norm2_shift,
    w_up,
    b_up,
    w_down,
    b_down,
    teacher,
    valid_mask,
    parents,
    summary,
):

    def attention_weights():
        return (
            lax.all_gather(w_query, "fsdp", axis=0, tiled=True),
            lax.all_gather(w_key, "fsdp", axis=0, tiled=True),
            lax.all_gather(w_value, "fsdp", axis=0, tiled=True),
            lax.all_gather(w_out, "fsdp", axis=0, tiled=True),
        )

    def feed_weights():
        return (
            lax.all_gather(w_up, "fsdp", axis=0, tiled=True),
            lax.all_gather(w_down, "fsdp", axis=0, tiled=True),
        )

    inputs = tokens.astype(jnp.float32)
    normed = layer_norm(inputs, norm1_gain, norm1_shift).astype(jnp.bfloat16)
    normed_all = lax.all_gather(normed, "tp", axis=0, tiled=True)
    full_query, full_key, full_value, full_out = attention_weights()
    queries = (
        (jnp.dot(normed_all, full_query, preferred_element_type=jnp.float32) + b_query) * 0.125
    ).astype(jnp.bfloat16)
    key_states = jnp.dot(normed_all, full_key, preferred_element_type=jnp.float32).astype(
        jnp.bfloat16
    )
    value_states = (
        jnp.dot(normed_all, full_value, preferred_element_type=jnp.float32) + b_value
    ).astype(jnp.bfloat16)
    tables = tree_tables(parents[0], summary[0], normed_all.shape[0])
    attended, log_totals = attend_forward(queries, key_states, value_states, tables)
    branch = lax.psum_scatter(
        contract(attended, full_out, 1, 1), "tp", scatter_dimension=0, tiled=True
    )
    hidden = inputs + branch + b_out
    normed_mid = layer_norm(hidden, norm2_gain, norm2_shift).astype(jnp.bfloat16)
    normed_mid_all = lax.all_gather(normed_mid, "tp", axis=0, tiled=True)
    full_up, full_down = feed_weights()
    active = jnp.maximum(
        jnp.dot(normed_mid_all, full_up, preferred_element_type=jnp.float32) + b_up, 0.0
    ).astype(jnp.bfloat16)
    feed_out = lax.psum_scatter(
        contract(active, full_down, 1, 1), "tp", scatter_dimension=0, tiled=True
    )
    output = hidden + feed_out + b_down
    weight_mask = valid_mask.astype(jnp.float32)
    deviation = output - teacher.astype(jnp.float32)
    valid_count, squares = lax.psum(
        (jnp.sum(weight_mask), jnp.sum(weight_mask[:, None] * deviation * deviation)),
        ("fsdp", "tp"),
    )
    mean_loss = squares / (valid_count * tokens.shape[1])
    total_tokens = tokens.shape[0] * lax.axis_size("fsdp") * lax.axis_size("tp")
    grad_output = 2.0 * total_tokens / valid_count * weight_mask[:, None] * deviation
    grad_feed_all = lax.all_gather(grad_output.astype(jnp.bfloat16), "tp", axis=0, tiled=True)
    full_up, full_down = feed_weights()
    grad_w_down = contract(grad_feed_all, active, 0, 0)
    grad_pre = jnp.where(
        active > 0, jnp.dot(grad_feed_all, full_down, preferred_element_type=jnp.float32), 0.0
    ).astype(jnp.bfloat16)
    grad_w_up = contract(normed_mid_all, grad_pre, 0, 0)
    grad_w_up, grad_w_down = (
        lax.psum_scatter(
            grad_w_up.astype(jnp.bfloat16), "fsdp", scatter_dimension=0, tiled=True
        ).astype(jnp.float32),
        lax.psum_scatter(
            grad_w_down.astype(jnp.bfloat16), "fsdp", scatter_dimension=0, tiled=True
        ).astype(jnp.float32),
    )
    grad_mid = lax.psum_scatter(
        contract(grad_pre, full_up, 1, 1), "tp", scatter_dimension=0, tiled=True
    )
    second_norm, second_pull = jax.vjp(layer_norm, hidden, norm2_gain, norm2_shift)
    grad_hidden_norm, grad_norm2_gain, grad_norm2_shift = second_pull(grad_mid)
    grad_hidden = grad_output + grad_hidden_norm
    grad_branch_all = lax.all_gather(grad_hidden.astype(jnp.bfloat16), "tp", axis=0, tiled=True)
    full_query, full_key, full_value, full_out = attention_weights()
    grad_w_out = contract(grad_branch_all, attended, 0, 0)
    grad_attended = jnp.dot(grad_branch_all, full_out, preferred_element_type=jnp.float32).astype(
        jnp.bfloat16
    )
    grad_queries, grad_keys, grad_values = attend_backward(
        queries, key_states, value_states, grad_attended, log_totals, tables
    )
    grad_pre_query = grad_queries * jnp.bfloat16(0.125)
    grad_w_query = contract(normed_all, grad_pre_query, 0, 0)
    grad_w_key = contract(normed_all, grad_keys, 0, 0)
    grad_w_value = contract(normed_all, grad_values, 0, 0)
    grad_w_query, grad_w_key, grad_w_value, grad_w_out = (
        lax.psum_scatter(grad_w_query, "fsdp", scatter_dimension=0, tiled=True),
        lax.psum_scatter(grad_w_key, "fsdp", scatter_dimension=0, tiled=True),
        lax.psum_scatter(grad_w_value, "fsdp", scatter_dimension=0, tiled=True),
        lax.psum_scatter(grad_w_out, "fsdp", scatter_dimension=0, tiled=True),
    )
    grad_normed = (
        contract(grad_pre_query, full_query, 1, 1)
        + contract(grad_keys, full_key, 1, 1)
        + contract(grad_values, full_value, 1, 1)
    )
    grad_normed = lax.psum_scatter(grad_normed, "tp", scatter_dimension=0, tiled=True)
    first_norm, first_pull = jax.vjp(layer_norm, inputs, norm1_gain, norm1_shift)
    grad_input_norm, grad_norm1_gain, grad_norm1_shift = first_pull(grad_normed)
    grad_tokens = grad_hidden + grad_input_norm
    column = lax.axis_index("tp")
    tp_count = lax.axis_size("tp")

    def widen(share_part):
        widened = jnp.zeros((share_part.shape[0] * tp_count,), jnp.float32)
        return lax.dynamic_update_slice_in_dim(widened, share_part, column * share_part.shape[0], 0)

    def narrow(widened, span_width):
        return lax.dynamic_slice_in_dim(widened, column * span_width, span_width, 0)

    summed = lax.psum(
        (
            grad_norm1_gain,
            grad_norm1_shift,
            widen(jnp.sum(grad_pre_query.astype(jnp.float32), axis=0)),
            widen(jnp.sum(grad_values.astype(jnp.float32), axis=0)),
            jnp.sum(grad_hidden, axis=0),
            grad_norm2_gain,
            grad_norm2_shift,
            widen(jnp.sum(grad_pre.astype(jnp.float32), axis=0)),
            jnp.sum(grad_output, axis=0),
        ),
        ("fsdp", "tp"),
    )
    return (
        output.astype(jnp.bfloat16),
        mean_loss,
        grad_tokens,
        summed[0],
        summed[1],
        grad_w_query,
        narrow(summed[2], b_query.shape[0]),
        grad_w_key,
        grad_w_value,
        narrow(summed[3], b_value.shape[0]),
        grad_w_out,
        summed[4],
        summed[5],
        summed[6],
        grad_w_up,
        narrow(summed[7], b_up.shape[0]),
        grad_w_down,
        summed[8],
    )


def solution(mesh):
    placed = (
        P(("fsdp", "tp"), None),
        P(),
        P(),
        P("fsdp", "tp"),
        P("tp"),
        P("fsdp", "tp"),
        P("fsdp", "tp"),
        P("tp"),
        P("fsdp", "tp"),
        P(),
        P(),
        P(),
        P("fsdp", "tp"),
        P("tp"),
        P("fsdp", "tp"),
        P(),
        P(("fsdp", "tp"), None),
        P(("fsdp", "tp")),
        P("fsdp", None),
        P("fsdp", None, None),
    )
    return jax.shard_map(
        body,
        mesh=mesh,
        in_specs=placed,
        out_specs=(
            P(("fsdp", "tp"), None),
            P(),
            P(("fsdp", "tp"), None),
            P(),
            P(),
            P("fsdp", "tp"),
            P("tp"),
            P("fsdp", "tp"),
            P("fsdp", "tp"),
            P("tp"),
            P("fsdp", "tp"),
            P(),
            P(),
            P(),
            P("fsdp", "tp"),
            P("tp"),
            P("fsdp", "tp"),
            P(),
        ),
        check_vma=False,
    )
```

profile of v0, /device:TPU:0, one launch (start us, length us, event | category | flops | bytes accessed | tf_op | source)
XLA Modules:
  0.0 1605.3 jit_solution(4273150163818574457)
XLA Ops:
  18.1 22.4 %all-gather.15.cloned.1.call-done = bf16[2048,512]{1,0:T(8,128)(2,1)} async-done(((bf16[256,512]{1,0:T(8,128)(2,1)}), bf16[2048,512]{1,0:T(8,128)(2,1)}) %all-gather.15.cloned.1.call-update) | async-done | bytes 2097168 | tf_op jit(solution)/shard_map/all_gather | solution.py:180
  40.6 82.9 %all-gather.11.cloned.1.call-done = bf16[1024,2048]{1,0:T(8,128)(2,1)} async-done(((bf16[256,2048]{1,0:T(8,128)(2,1)}), bf16[1024,2048]{1,0:T(8,128)(2,1)}) %all-gather.11.cloned.1.call-update) | async-done | bytes 4194320 | tf_op jit(solution)/shard_map/all_gather | solution.py:193
  123.5 5.2 convolution_convert_fusion.4
  128.7 22.9 %all-gather.17.cloned.1.call-done = bf16[2048,512]{1,0:T(8,128)(2,1)} async-done(((bf16[256,512]{1,0:T(8,128)(2,1)}), bf16[2048,512]{1,0:T(8,128)(2,1)}) %all-gather.17.cloned.1.call-update) | async-done | bytes 2097168 | tf_op jit(solution)/shard_map/all_gather | solution.py:181
  151.7 6.2 add_convert_fusion.1
  157.9 23.3 %all-gather.13.cloned.1.call-done = bf16[2048,512]{1,0:T(8,128)(2,1)} async-done(((bf16[256,512]{1,0:T(8,128)(2,1)}), bf16[2048,512]{1,0:T(8,128)(2,1)}) %all-gather.13.cloned.1.call-update) | async-done | bytes 2097168 | tf_op jit(solution)/shard_map/all_gather | solution.py:179
  181.2 5.2 multiply_convert_fusion.1
  187.5 34.3 %while.45 = (s32[]{:T(128)}, bf16[2,512,8,64]{1,3,2,0:T(8,128)(2,1)}, f32[2,8,512]{2,1,0:T(8,128)S(1)}, s32[2]{0:T(128)S(1)}, bf16[8,8]{1,0:T(8,128)(2,1)S(1)}, ...) while((s32[]{:T(128)}, ...), condition=%wide.region_9.10_spmd.clone, body=%wide.region_6.9_spmd.clone.sunk | while | flops 1123386368 | bytes 68315536 | solution.py:99
  192.1 2.9 select_reduce_fusion.2
  195.0 3.8 fusion.182
  198.8 5.0 fusion.183
  209.2 2.9 select_reduce_fusion.2
  212.1 3.8 fusion.182
  215.9 5.0 fusion.183
  221.9 2.7 copy.41
  224.9 7.6 fusion.97
  233.3 144.0 %reduce-scatter.11.cloned.1.call-done = f32[256,2048]{1,0:T(8,128)} async-done(((f32[1024,2048]{1,0:T(8,128)}), f32[256,2048]{1,0:T(8,128)}) %reduce-scatter.11.cloned.1.call-update) | async-done | bytes 2097168 | tf_op jit(solution)/shard_map/reduce_scatter | solution.py:206
  382.4 51.6 %all-gather.23.cloned.1.call-done = bf16[2048,2048]{1,0:T(8,128)(2,1)} async-done(((bf16[256,2048]{1,0:T(8,128)(2,1)}), bf16[2048,2048]{1,0:T(8,128)(2,1)}) %all-gather.23.cloned.1.call-update) | async-done | bytes 8388624 | tf_op jit(solution)/shard_map/all_gather | solution.py:187
  434.0 82.9 %all-gather.21.cloned.1.call-done = bf16[1024,2048]{1,0:T(8,128)(2,1)} async-done(((bf16[256,2048]{1,0:T(8,128)(2,1)}), bf16[1024,2048]{1,0:T(8,128)(2,1)}) %all-gather.21.cloned.1.call-update) | async-done | bytes 4194320 | tf_op jit(solution)/shard_map/all_gather | solution.py:211
  517.0 14.1 maximum_convert_fusion
  531.0 40.6 %all-gather.25.cloned.1.call-done = bf16[2048,2048]{1,0:T(8,128)(2,1)} async-done(((bf16[256,2048]{1,0:T(8,128)(2,1)}), bf16[2048,2048]{1,0:T(8,128)(2,1)}) %all-gather.25.cloned.1.call-update) | async-done | bytes 8388624 | tf_op jit(solution)/shard_map/all_gather | solution.py:188
  571.6 14.6 fusion.98
  587.5 44.5 %psum.78 = f32[]{:T(128)} all-reduce(f32[]{:T(128)} %convert_reduce_fusion.5), channel_id=1, replica_groups=mesh['fsdp'=8,'tp'=4] {'fsdp','tp'}, use_global_device_ids=true, to_apply=%region_17.18 | all-reduce | flops 1 | bytes 8 | tf_op jit(solution)/shard_map/psum | solution.py:222
  632.7 99.3 %reduce-scatter.13.cloned.1.call-done = f32[256,2048]{1,0:T(8,128)} async-done(((f32[1024,2048]{1,0:T(8,128)}), f32[256,2048]{1,0:T(8,128)}) %reduce-scatter.13.cloned.1.call-update) | async-done | bytes 2097168 | tf_op jit(solution)/shard_map/reduce_scatter | solution.py:216
  732.1 4.5 multiply_convert_fusion.2
  736.7 81.4 %all-gather.27.cloned.1.call-done = bf16[1024,2048]{1,0:T(8,128)(2,1)} async-done(((bf16[256,2048]{1,0:T(8,128)(2,1)}), bf16[1024,2048]{1,0:T(8,128)(2,1)}) %all-gather.27.cloned.1.call-update) | async-done | bytes 4194320 | tf_op jit(solution)/shard_map/all_gather | solution.py:229
  818.1 14.2 convert_reduce_fusion
  834.3 13.3 fusion.99
  847.7 143.2 %reduce-scatter.15.cloned.1.call-done = f32[256,2048]{1,0:T(8,128)} async-done(((f32[1024,2048]{1,0:T(8,128)}), f32[256,2048]{1,0:T(8,128)}) %reduce-scatter.15.cloned.1.call-update) | async-done | bytes 2097168 | tf_op jit(solution)/shard_map/reduce_scatter | solution.py:244
  990.9 3.0 multiply_reduce_fusion.1
  999.8 14.2 convolution_convert_fusion.2
  1014.1 14.1 convolution_convert_fusion.1
  1028.2 53.0 %all-gather.29.cloned.1.call-done = bf16[1024,2048]{1,0:T(8,128)(2,1)} async-done(((bf16[256,2048]{1,0:T(8,128)(2,1)}), bf16[1024,2048]{1,0:T(8,128)(2,1)}) %all-gather.29.cloned.1.call-update) | async-done | bytes 4194320 | tf_op jit(solution)/shard_map/all_gather | solution.py:250
  1081.2 6.2 convolution_convert_fusion.3
  1088.5 104.5 %while.47 = (s32[]{:T(128)}, f32[1024,8,64]{0,2,1:T(8,128)S(1)}, f32[1024,8,64]{0,2,1:T(8,128)}, bf16[2,512,8,64]{1,3,2,0:T(8,128)(2,1)}, s32[2]{0:T(128)S(1)}, ...) while((s32[]{:T(128)}, f32[1024,8,64]{0,2,1:T(8,128)S(1)}, ...), condition=%wide.region_23.24_spmd.clone, body=%wide.region_21.23_spmd.clone.sunk | while | flops 2748679168 | bytes 224012784 | solution.py:143
  1094.0 3.8 fusion.198
  1097.8 6.0 copy-done
  1103.8 5.7 bitcast_add_fusion.5
  1109.5 12.6 multiply_reduce_fusion.6
  1122.1 12.6 multiply_convert_fusion.4
  1134.7 2.7 fusion.200
  1144.6 3.6 fusion.198
  1148.2 5.8 copy-done
  1153.9 6.1 bitcast_add_fusion.5
  1160.0 15.1 multiply_reduce_fusion.6
  1175.2 12.8 multiply_convert_fusion.4
  1188.0 2.7 fusion.200
  1197.8 2.4 fusion.101
  1200.2 2.4 fusion.100
  1202.6 5.7 add_add_fusion
  1209.6 6.6 fusion.105
  1216.4 6.6 fusion.104
  1224.3 6.5 fusion.103
  1230.9 6.5 fusion.102
  1238.4 2.8 convert_element_type.150
  1241.3 2.9 convert_element_type.153
  1245.1 131.1 %reduce-scatter.17.cloned.1.call-done = f32[256,2048]{1,0:T(8,128)} async-done(((f32[1024,2048]{1,0:T(8,128)}), f32[256,2048]{1,0:T(8,128)}) %reduce-scatter.17.cloned.1.call-update) | async-done | bytes 2097168 | tf_op jit(solution)/shard_map/reduce_scatter | solution.py:274
  1376.3 2.3 fusion.92
  1379.6 43.3 %all-reduce.2 = (f32[]{:T(128)}, f32[2048]{0:T(1024)}, f32[2048]{0:T(1024)}, f32[2048]{0:T(1024)S(1)}, f32[2048]{0:T(1024)S(1)}, /*index=5*/f32[2048]{0:T(1024)}...) all-reduce(f32[]{:T(128)} %get-tuple-element.546, ...), channel_id=1, replica_groups=mesh['fsdp'=8,'tp'=4] {'fsdp','tp'}, use_global_device_ids=true, to_apply=%region_15.16 | all-reduce | flops 24577 | bytes 196616 | tf_op jit(solution)/shard_map/psum | solution.py:222
  1425.5 3.6 add_add_fusion.3
  1429.1 3.0 reduce-scatter.25.cloned.1.call-done
  1432.0 55.0 %reduce-scatter.23.cloned.1.call-done = f32[256,512]{1,0:T(8,128)} async-done(((f32[2048,512]{1,0:T(8,128)}), f32[256,512]{1,0:T(8,128)}) %reduce-scatter.23.cloned.1.call-update) | async-done | bytes 524304 | tf_op jit(solution)/shard_map/reduce_scatter | solution.py:266
  1487.0 55.1 %reduce-scatter.21.cloned.1.call-done = f32[256,512]{1,0:T(8,128)} async-done(((f32[2048,512]{1,0:T(8,128)}), f32[256,512]{1,0:T(8,128)}) %reduce-scatter.21.cloned.1.call-update) | async-done | bytes 524304 | tf_op jit(solution)/shard_map/reduce_scatter | solution.py:265
  1542.1 55.0 %reduce-scatter.19.cloned.1.call-done = f32[256,512]{1,0:T(8,128)} async-done(((f32[2048,512]{1,0:T(8,128)}), f32[256,512]{1,0:T(8,128)}) %reduce-scatter.19.cloned.1.call-update) | async-done | bytes 524304 | tf_op jit(solution)/shard_map/reduce_scatter | solution.py:264
  (260 shorter events, 59.4 us)
Async XLA Ops:
  7.2 5.1 copy-start.5
  7.2 5.1 copy-start.24
  7.2 5.1 copy-start.37
  7.2 33.3 %all-gather.15.cloned.1.call-start = ((), (), s32[]{:S(2)}) async-start(), calls=%async_computation.12 | async-start | bytes 2359296 | tf_op jit(solution)/shard_map/all_gather | solution.py:180
  8.0 115.5 %all-gather.11.cloned.1.call-start = ((), (), s32[]{:S(2)}) async-start(), calls=%async_computation.10 | async-start | bytes 5242880 | tf_op jit(solution)/shard_map/all_gather | solution.py:193
  9.5 2.2 copy-start.27
  11.7 4.0 copy-start.49
  11.7 6.3 copy-start.42
  13.7 137.9 %all-gather.17.cloned.1.call-start = ((), (), s32[]{:S(2)}) async-start(), calls=%async_computation.13 | async-start | bytes 2359296 | tf_op jit(solution)/shard_map/all_gather | solution.py:181
  14.5 166.8 %all-gather.13.cloned.1.call-start = ((), (), s32[]{:S(2)}) async-start(), calls=%async_computation.11 | async-start | bytes 2359296 | tf_op jit(solution)/shard_map/all_gather | solution.py:179
  15.0 209.8 %all-gather.19.cloned.1.call-start = ((), (), s32[]{:S(2)}) async-start(), calls=%async_computation.14 | async-start | bytes 2359296 | tf_op jit(solution)/shard_map/all_gather | solution.py:182
  15.6 361.6 %reduce-scatter.11.cloned.1.call-start = ((), (), s32[]{:S(2)}) async-start(), calls=%async_computation.15 | async-start | bytes 10485760 | tf_op jit(solution)/shard_map/reduce_scatter | solution.py:206
  18.1 133.5 %copy-start.47 = (f32[512]{0:T(512)S(1)}, f32[512]{0:T(512)}, u32[]{:S(2)}) copy-start(f32[512]{0:T(512)} %param.33) | copy-start | bytes 6148
  128.7 52.5 %copy-start.48 = (f32[512]{0:T(512)S(1)}, f32[512]{0:T(512)}, u32[]{:S(2)}) copy-start(f32[512]{0:T(512)} %param.30) | copy-start | bytes 6148
  195.0 3.8 copy-start.7
  195.0 3.8 copy-start.17
  212.1 3.8 copy-start.7
  212.1 3.8 copy-start.17
  221.9 10.6 copy-start.3
  224.8 7.6 copy-start.22
  232.4 144.8 %copy-start.38 = (f32[2048]{0:T(1024)S(1)}, f32[2048]{0:T(1024)}, u32[]{:S(2)}) copy-start(f32[2048]{0:T(1024)} %param.35) | copy-start | bytes 24580
  232.5 201.6 %all-gather.23.cloned.1.call-start = ((), (), s32[]{:S(2)}) async-start(), calls=%async_computation.17 | async-start | bytes 9437184 | tf_op jit(solution)/shard_map/all_gather | solution.py:187
  233.2 283.7 %all-gather.21.cloned.1.call-start = ((), (), s32[]{:S(2)}) async-start(), calls=%async_computation.16 | async-start | bytes 5242880 | tf_op jit(solution)/shard_map/all_gather | solution.py:211
  380.2 136.8 %copy-start.46 = (f32[2048]{0:T(1024)S(1)}, f32[2048]{0:T(1024)}, u32[]{:S(2)}) copy-start(f32[2048]{0:T(1024)} %param.39) | copy-start | bytes 24580
  381.6 190.0 %all-gather.25.cloned.1.call-start = ((), (), s32[]{:S(2)}) async-start(), calls=%async_computation.18 | async-start | bytes 9437184 | tf_op jit(solution)/shard_map/all_gather | solution.py:188
  382.4 349.7 %reduce-scatter.13.cloned.1.call-start = ((), (), s32[]{:S(2)}) async-start(), calls=%async_computation.19 | async-start | bytes 10485760 | tf_op jit(solution)/shard_map/reduce_scatter | solution.py:216
  586.2 145.8 %copy-start.41 = (f32[2048]{0:T(1024)S(1)}, f32[2048]{0:T(1024)}, u32[]{:S(2)}) copy-start(f32[2048]{0:T(1024)} %param.41) | copy-start | bytes 24580
  586.3 231.8 %all-gather.27.cloned.1.call-start = ((), (), s32[]{:S(2)}) async-start(), calls=%async_computation.20 | async-start | bytes 5242880 | tf_op jit(solution)/shard_map/all_gather | solution.py:229
  736.6 254.3 %reduce-scatter.15.cloned.1.call-start = ((), (), s32[]{:S(2)}) async-start(), calls=%async_computation.21 | async-start | bytes 10485760 | tf_op jit(solution)/shard_map/reduce_scatter | solution.py:244
  832.3 2.0 copy-start.50
  847.6 233.6 %all-gather.29.cloned.1.call-start = ((), (), s32[]{:S(2)}) async-start(), calls=%async_computation.22 | async-start | bytes 5242880 | tf_op jit(solution)/shard_map/all_gather | solution.py:250
  990.9 3.1 copy-start.15
  994.0 1.6 copy-start.16
  999.7 238.7 %reduce-scatter.27.cloned.1.call-start = ((), (), s32[]{:S(2)}) async-start(), calls=%async_computation.28 | async-start | bytes 9437184 | tf_op jit(solution)/shard_map/reduce_scatter | solution.py:237
  1014.0 227.3 %reduce-scatter.29.cloned.1.call-start = ((), (), s32[]{:S(2)}) async-start(), calls=%async_computation.29 | async-start | bytes 9437184 | tf_op jit(solution)/shard_map/reduce_scatter | solution.py:240
  1028.2 348.1 %reduce-scatter.17.cloned.1.call-start = ((), (), s32[]{:S(2)}) async-start(), calls=%async_computation.23 | async-start | bytes 10485760 | tf_op jit(solution)/shard_map/reduce_scatter | solution.py:274
  1094.0 9.8 copy-start.1
  1097.8 6.0 copy-start
  1122.0 12.6 copy-start.11
  1134.7 2.7 copy-start.4
  1137.4 1.9 copy-start.12
  1144.6 9.4 copy-start.1
  1148.1 5.8 copy-start
  1175.2 12.8 copy-start.11
  1188.0 2.7 copy-start.4
  1190.6 2.0 copy-start.12
  1193.1 1.5 copy-start.13
  1193.3 3.5 copy-start.20
  1194.7 1.8 copy-start.2
  1196.1 1.7 copy-start.44
  1197.8 2.4 copy-start.45
  1200.2 2.4 copy-start.19
  1208.4 223.7 %reduce-scatter.25.cloned.1.call-start = ((), (), s32[]{:S(2)}) async-start(), calls=%async_computation.27 | async-start | bytes 4718592 | tf_op jit(solution)/shard_map/reduce_scatter | solution.py:267
  1216.2 270.8 %reduce-scatter.23.cloned.1.call-start = ((), (), s32[]{:S(2)}) async-start(), calls=%async_computation.26 | async-start | bytes 4718592 | tf_op jit(solution)/shard_map/reduce_scatter | solution.py:266
  1223.0 319.1 %reduce-scatter.21.cloned.1.call-start = ((), (), s32[]{:S(2)}) async-start(), calls=%async_computation.25 | async-start | bytes 4718592 | tf_op jit(solution)/shard_map/reduce_scatter | solution.py:265
  1230.8 366.3 %reduce-scatter.19.cloned.1.call-start = ((), (), s32[]{:S(2)}) async-start(), calls=%async_computation.24 | async-start | bytes 4718592 | tf_op jit(solution)/shard_map/reduce_scatter | solution.py:264
  1241.2 3.0 copy-start.14
  1241.3 135.0 %copy-start.6 = (bf16[256,2048]{1,0:T(8,128)(2,1)S(1)}, bf16[256,2048]{1,0:T(8,128)(2,1)}, u32[]{:S(2)}) copy-start(bf16[256,2048]{1,0:T(8,128)(2,1)} %param.26) | copy-start | bytes 3145732
  1241.3 135.0 %copy-start.25 = (f32[2048]{0:T(1024)S(1)}, f32[2048]{0:T(1024)}, u32[]{:S(2)}) copy-start(f32[2048]{0:T(1024)} %param.27) | copy-start | bytes 24580
  1241.3 135.0 %copy-start.28 = (f32[256]{0:T(256)S(1)}, f32[256]{0:T(256)}, u32[]{:S(2)}) copy-start(f32[256]{0:T(256)} %copy-done.27) | copy-start | bytes 3076
  1244.2 134.4 %copy-start.36 = (f32[256]{0:T(256)S(1)}, f32[256]{0:T(256)}, u32[]{:S(2)}) copy-start(f32[256]{0:T(256)} %copy-done.35) | copy-start | bytes 3076
  1244.2 134.4 %copy-start.34 = (f32[256]{0:T(256)S(1)}, f32[256]{0:T(256)}, u32[]{:S(2)}) copy-start(f32[256]{0:T(256)} %copy-done.33) | copy-start | bytes 3076
  1376.3 2.4 copy-start.10
  1378.6 46.9 %copy-start.9 = (f32[256,2048]{1,0:T(8,128)S(1)}, f32[256,2048]{1,0:T(8,128)}, u32[]{:S(2)}) copy-start(f32[256,2048]{1,0:T(8,128)} %copy-done.8) | copy-start | bytes 6291460
  (15 other events, 13.9 us)
Sparse Core Ops, SparseCore 0:
  9.9 30.5 all-gather.14
  42.7 80.7 all-gather.10
  125.4 26.2 all-gather.16
  153.4 27.7 all-gather.12
  183.0 27.7 all-gather.18
  232.6 144.6 reduce-scatter.10
  379.1 54.8 all-gather.22
  436.2 80.7 all-gather.20
  518.9 52.7 all-gather.24
  586.4 145.6 reduce-scatter.12
  736.7 81.2 all-gather.26
  847.8 143.0 reduce-scatter.14
  999.8 81.3 all-gather.28
  1084.6 69.9 reduce-scatter.26
  1157.9 71.4 reduce-scatter.28
  1231.6 144.6 reduce-scatter.16
  1380.0 51.9 reduce-scatter.24
  1435.8 51.1 reduce-scatter.22
  1490.9 51.1 reduce-scatter.20
  1545.9 51.1 reduce-scatter.18
where the time goes:
time: 1610 us
  waiting for transfers between devices  1150 us (71%)
  matrix products  230 us (14%)
  blocking collectives  87.8 us (5%)
  other arithmetic  71.4 us (4%)
  local copies, waits for them, and re-layouts  37 us (2%)
  between operations  18.2 us (1%)
    reduce_scatter x1, waiting for transfers between devices, body(): lax.psum_scatter(contract(attended, full_out, 1, 1), 'tp', scatter_dimens...  144 us
    reduce_scatter x1, waiting for transfers between devices, body(): lax.psum_scatter(contract(grad_pre, full_up, 1, 1), 'tp', scatter_dimensi...  143 us
    reduce_scatter x1, waiting for transfers between devices, body(): lax.psum_scatter(grad_normed, 'tp', scatter_dimension=0, tiled=True)  131 us
    dot_general x12, matrix products, contract(): lax.dot_general(left_side, right_side, (((left_dim,), (right_dim,)), ((),...  101 us
    reduce_scatter x1, waiting for transfers between devices, body(): lax.psum_scatter(contract(active, full_down, 1, 1), 'tp', scatter_dimensi...  99.3 us
    psum x2, blocking collectives, body(): lax.psum((jnp.sum(weight_mask), jnp.sum(weight_mask[:, None] * deviation...  87.8 us
    all_gather x1, waiting for transfers between devices, body(): normed_all = lax.all_gather(normed, 'tp', axis=0, tiled=True)  82.9 us
    all_gather x1, waiting for transfers between devices, body(): normed_mid_all = lax.all_gather(normed_mid, 'tp', axis=0, tiled=True)  82.9 us
  transfers between devices with their start and end apart: 20, of which 17 were waited for; matrix products, arithmetic and copies ran while one was open for 16% of the time, Pallas kernels for 0%

commit v1 on v0

--- a/solution.py
+++ b/solution.py
@@ -1,3 +1,4 @@
+import functools
 import jax
 import jax.numpy as jnp
 from jax import lax
@@ -6,6 +7,39 @@
 HD = 64
 EPSILON = 1e-05
 MASKED_SCORE = -1e30
+
+
+def register_threads(obj, axis_no):
+    obj = jnp.moveaxis(obj, 0, axis_no)
+    long_array = obj.shape
+    return obj.reshape(
+        *long_array[:axis_no],
+        long_array[axis_no] * long_array[axis_no + 1],
+        *long_array[axis_no + 2 :]
+    )
+
+
+def _close_panel(x_in, shard_axis, row_dim):
+    cores_n = lax.axis_size(shard_axis)
+    all_rows = list(map(lambda ix: (ix, (ix + 1) % cores_n), range(cores_n)))
+    found = [(j, dd) for dd, j in all_rows]
+    y2, inter = ([], [])
+    k = 0
+    while k < cores_n - 1:
+        if k % 2 == 0:
+            y2.append(lax.ppermute(y2[-1] if y2 else x_in, shard_axis, all_rows))
+        else:
+            current_block = lax.ppermute(inter[-1] if inter else x_in, shard_axis, found)
+            inter.append(current_block)
+        k = k + 1
+    low = jnp.stack([*y2[::-1], x_in, *inter])
+    w2 = lax.axis_index(shard_axis)
+    d_next = w2 - len(y2)
+    low = low[(jnp.arange(cores_n) - d_next) % cores_n]
+    return register_threads(low, row_dim)
+
+
+_define_roads = functools.partial(_close_panel, shard_axis="fsdp", row_dim=0)
 
 
 def layer_norm(vectors, norm_gain, norm_shift):
@@ -183,10 +217,7 @@
         )
 
     def feed_weights():
-        return (
-            lax.all_gather(w_up, "fsdp", axis=0, tiled=True),
-            lax.all_gather(w_down, "fsdp", axis=0, tiled=True),
-        )
+        return (_define_roads(w_up), lax.all_gather(w_down, "fsdp", axis=0, tiled=True))
 
     inputs = tokens.astype(jnp.float32)
     normed = layer_norm(inputs, norm1_gain, norm1_shift).astype(jnp.bfloat16)

time: 1610 us -> 1560 us (0.969)
  waiting for transfers between devices: 1150 us -> 1060 us
  local copies, waits for them, and re-layouts: 37 us -> 57.3 us
    ppermute x0 -> x7, waiting for transfers between devices: none -> 85.1 us  [the longest x4 85.1 us: _close_panel(): y2.append(lax.ppermute(y2[-1] if y2 else x_in, shard_axis, all_rows))]
    all_gather x1, waiting for transfers between devices: 82.9 us -> 0.01 us  [body(): normed_mid_all = lax.all_gather(normed_mid, 'tp', axis=0, tiled=True)]
    all_gather x1 -> x0, waiting for transfers between devices: 51.6 us -> none  [feed_weights(): lax.all_gather(w_up, 'fsdp', axis=0, tiled=True)]
    all_gather x1, waiting for transfers between devices: 40.6 us -> 5.61 us  [feed_weights(): lax.all_gather(w_down, 'fsdp', axis=0, tiled=True)]
  transfers between devices with their start and end apart: 20 -> 26, of which waited for: 17 -> 19; matrix products, arithmetic and copies ran while one was open for 16% -> 18% of each run, Pallas kernels for 0% -> 0%
where the time goes in v1:
time: 1560 us; the launch traced here: 1550 us
  waiting for transfers between devices  1060 us (68%)
  matrix products  230 us (15%)
  blocking collectives  87.7 us (6%)
  other arithmetic  75.2 us (5%)
  local copies, waits for them, and re-layouts  57.3 us (4%)
  between operations  18.2 us (1%)
    reduce_scatter x1, waiting for transfers between devices, body(): lax.psum_scatter(contract(attended, full_out, 1, 1), 'tp', scatter_dimens...  145 us
    reduce_scatter x1, waiting for transfers between devices, body(): lax.psum_scatter(contract(grad_pre, full_up, 1, 1), 'tp', scatter_dimensi...  143 us
    reduce_scatter x1, waiting for transfers between devices, body(): lax.psum_scatter(grad_normed, 'tp', scatter_dimension=0, tiled=True)  130 us
    dot_general x12, matrix products, contract(): lax.dot_general(left_side, right_side, (((left_dim,), (right_dim,)), ((),...  101 us
    reduce_scatter x1, waiting for transfers between devices, body(): lax.psum_scatter(contract(active, full_down, 1, 1), 'tp', scatter_dimensi...  99.3 us
    psum x2, blocking collectives, body(): lax.psum((jnp.sum(weight_mask), jnp.sum(weight_mask[:, None] * deviation...  87.7 us
    ppermute x4, waiting for transfers between devices, _close_panel(): y2.append(lax.ppermute(y2[-1] if y2 else x_in, shard_axis, all_rows))  85.1 us
    all_gather x1, waiting for transfers between devices, body(): normed_all = lax.all_gather(normed, 'tp', axis=0, tiled=True)  82.9 us
  transfers between devices with their start and end apart: 26, of which 19 were waited for; matrix products, arithmetic and copies ran while one was open for 18% of the time, Pallas kernels for 0%

profile of v1, /device:TPU:0, one launch (start us, length us, event | category | flops | bytes accessed | tf_op | source)
XLA Modules:
  0.0 1551.0 jit_solution(291893287170971777)
XLA Ops:
  12.3 2.7 fusion.79
  19.4 21.2 %all-gather.14.cloned.1.call-done = bf16[2048,512]{1,0:T(8,128)(2,1)} async-done(((bf16[256,512]{1,0:T(8,128)(2,1)}), bf16[2048,512]{1,0:T(8,128)(2,1)}) %all-gather.14.cloned.1.call-update) | async-done | bytes 2097168 | tf_op jit(solution)/shard_map/all_gather | solution.py:214
  40.5 82.9 %all-gather.10.cloned.1.call-done = bf16[1024,2048]{1,0:T(8,128)(2,1)} async-done(((bf16[256,2048]{1,0:T(8,128)(2,1)}), bf16[1024,2048]{1,0:T(8,128)(2,1)}) %all-gather.10.cloned.1.call-update) | async-done | bytes 4194320 | tf_op jit(solution)/shard_map/all_gather | solution.py:224
  123.4 5.2 convolution_convert_fusion.4
  128.7 22.9 %all-gather.16.cloned.1.call-done = bf16[2048,512]{1,0:T(8,128)(2,1)} async-done(((bf16[256,512]{1,0:T(8,128)(2,1)}), bf16[2048,512]{1,0:T(8,128)(2,1)}) %all-gather.16.cloned.1.call-update) | async-done | bytes 2097168 | tf_op jit(solution)/shard_map/all_gather | solution.py:215
  151.6 6.2 add_convert_fusion.1
  157.9 23.3 %all-gather.12.cloned.1.call-done = bf16[2048,512]{1,0:T(8,128)(2,1)} async-done(((bf16[256,512]{1,0:T(8,128)(2,1)}), bf16[2048,512]{1,0:T(8,128)(2,1)}) %all-gather.12.cloned.1.call-update) | async-done | bytes 2097168 | tf_op jit(solution)/shard_map/all_gather | solution.py:213
  181.2 5.2 multiply_convert_fusion.1
  187.5 34.4 %while.45 = (s32[]{:T(128)}, bf16[2,512,8,64]{1,3,2,0:T(8,128)(2,1)}, f32[2,8,512]{2,1,0:T(8,128)S(1)}, s32[2]{0:T(128)S(1)}, bf16[8,8]{1,0:T(8,128)(2,1)S(1)}, ...) while((s32[]{:T(128)}, ...), condition=%wide.region_9.10_spmd.clone, body=%wide.region_6.9_spmd.clone.sunk | while | flops 1123386368 | bytes 68315536 | solution.py:133
  192.1 2.9 select_reduce_fusion.2
  195.0 3.8 fusion.184
  198.8 5.0 fusion.185
  209.2 2.9 select_reduce_fusion.2
  212.1 3.8 fusion.184
  215.9 5.0 fusion.185
  221.9 3.1 copy.41
  225.3 7.6 fusion.99
  233.1 144.7 %reduce-scatter.11.cloned.1.call-done = f32[256,2048]{1,0:T(8,128)} async-done(((f32[1024,2048]{1,0:T(8,128)}), f32[256,2048]{1,0:T(8,128)}) %reduce-scatter.11.cloned.1.call-update) | async-done | bytes 2097168 | tf_op jit(solution)/shard_map/reduce_scatter | solution.py:237
  382.4 15.1 collective-permute-done
  400.2 22.8 %collective-permute-done.1 = bf16[256,2048]{1,0:T(8,128)(2,1)S(1)} collective-permute-done((bf16[256,2048]{1,0:T(8,128)(2,1)S(1)}, bf16[256,2048]{1,0:T(8,128)(2,1)S(1)}, u32[]{:S(2)}, u32[]{:S(2)}) %collective-permute-start.1) | collective-permute-done | bytes 1048608 | tf_op jit(solution)/shard_map/ppermute | solution.py:30
  425.7 23.2 %collective-permute-done.2 = bf16[256,2048]{1,0:T(8,128)(2,1)} collective-permute-done((bf16[256,2048]{1,0:T(8,128)(2,1)S(1)}, bf16[256,2048]{1,0:T(8,128)(2,1)}, u32[]{:S(2)}, u32[]{:S(2)}) %collective-permute-start.2) | collective-permute-done | bytes 1048608 | tf_op jit(solution)/shard_map/ppermute | solution.py:30
  449.0 2.9 collective-permute-start.6
  451.9 24.0 %collective-permute-done.3 = bf16[256,2048]{1,0:T(8,128)(2,1)} collective-permute-done((bf16[256,2048]{1,0:T(8,128)(2,1)}, bf16[256,2048]{1,0:T(8,128)(2,1)}, u32[]{:S(2)}, u32[]{:S(2)}) %collective-permute-start.3) | collective-permute-done | bytes 1048608 | tf_op jit(solution)/shard_map/ppermute | solution.py:30
  489.4 9.1 gather_fusion
  498.5 14.0 maximum_convert_fusion
  512.5 5.6 all-gather.22.cloned.1.call-done
  518.1 14.7 fusion.100
  534.1 44.5 %psum.78 = f32[]{:T(128)} all-reduce(f32[]{:T(128)} %convert_reduce_fusion.5), channel_id=1, replica_groups=mesh['fsdp'=8,'tp'=4] {'fsdp','tp'}, use_global_device_ids=true, to_apply=%region_17.18 | all-reduce | flops 1 | bytes 8 | tf_op jit(solution)/shard_map/psum | solution.py:253
  579.3 99.3 %reduce-scatter.13.cloned.1.call-done = f32[256,2048]{1,0:T(8,128)} async-done(((f32[1024,2048]{1,0:T(8,128)}), f32[256,2048]{1,0:T(8,128)}) %reduce-scatter.13.cloned.1.call-update) | async-done | bytes 2097168 | tf_op jit(solution)/shard_map/reduce_scatter | solution.py:247
  678.6 4.2 multiply_convert_fusion.2
  683.3 81.0 %all-gather.24.cloned.1.call-done = bf16[1024,2048]{1,0:T(8,128)(2,1)} async-done(((bf16[256,2048]{1,0:T(8,128)(2,1)}), bf16[1024,2048]{1,0:T(8,128)(2,1)}) %all-gather.24.cloned.1.call-update) | async-done | bytes 4194320 | tf_op jit(solution)/shard_map/all_gather | solution.py:260
  764.3 13.8 convert_reduce_fusion
  780.2 13.4 fusion.101
  793.6 143.2 %reduce-scatter.15.cloned.1.call-done = f32[256,2048]{1,0:T(8,128)} async-done(((f32[1024,2048]{1,0:T(8,128)}), f32[256,2048]{1,0:T(8,128)}) %reduce-scatter.15.cloned.1.call-update) | async-done | bytes 2097168 | tf_op jit(solution)/shard_map/reduce_scatter | solution.py:275
  936.8 3.0 multiply_reduce_fusion.1
  945.8 14.1 convolution_convert_fusion.2
  960.0 14.1 convolution_convert_fusion.1
  974.2 52.9 %all-gather.26.cloned.1.call-done = bf16[1024,2048]{1,0:T(8,128)(2,1)} async-done(((bf16[256,2048]{1,0:T(8,128)(2,1)}), bf16[1024,2048]{1,0:T(8,128)(2,1)}) %all-gather.26.cloned.1.call-update) | async-done | bytes 4194320 | tf_op jit(solution)/shard_map/all_gather | solution.py:281
  1027.1 6.2 convolution_convert_fusion.3
  1034.4 104.6 %while.47 = (s32[]{:T(128)}, f32[1024,8,64]{0,2,1:T(8,128)S(1)}, f32[1024,8,64]{0,2,1:T(8,128)}, bf16[2,512,8,64]{1,3,2,0:T(8,128)(2,1)}, s32[2]{0:T(128)S(1)}, ...) while((s32[]{:T(128)}, f32[1024,8,64]{0,2,1:T(8,128)S(1)}, ...), condition=%wide.region_23.24_spmd.clone, body=%wide.region_21.23_spmd.clone.sunk | while | flops 2748679168 | bytes 224012784 | solution.py:177
  1039.9 3.8 fusion.200
  1043.7 6.0 copy-done
  1049.7 5.7 bitcast_add_fusion.5
  1055.4 12.6 multiply_reduce_fusion.6
  1068.0 12.6 multiply_convert_fusion.4
  1090.5 3.6 fusion.200
  1094.1 5.8 copy-done
  1099.9 6.1 bitcast_add_fusion.5
  1106.0 15.2 multiply_reduce_fusion.6
  1121.1 12.8 multiply_convert_fusion.4
  1147.8 5.8 add_add_fusion
  1154.8 6.7 fusion.107
  1161.7 6.6 fusion.106
  1169.6 6.6 fusion.105
  1176.3 6.5 fusion.104
  1184.0 2.9 convert_element_type.150
  1186.9 2.8 convert_element_type.153
  1192.0 130.4 %reduce-scatter.17.cloned.1.call-done = f32[256,2048]{1,0:T(8,128)} async-done(((f32[1024,2048]{1,0:T(8,128)}), f32[256,2048]{1,0:T(8,128)}) %reduce-scatter.17.cloned.1.call-update) | async-done | bytes 2097168 | tf_op jit(solution)/shard_map/reduce_scatter | solution.py:305
  1325.7 43.1 %all-reduce.2 = (f32[]{:T(128)}, f32[2048]{0:T(1024)}, f32[2048]{0:T(1024)}, f32[2048]{0:T(1024)S(1)}, f32[2048]{0:T(1024)S(1)}, /*index=5*/f32[2048]{0:T(1024)}...) all-reduce(f32[]{:T(128)} %get-tuple-element.546, ...), channel_id=1, replica_groups=mesh['fsdp'=8,'tp'=4] {'fsdp','tp'}, use_global_device_ids=true, to_apply=%region_15.16 | all-reduce | flops 24577 | bytes 196616 | tf_op jit(solution)/shard_map/psum | solution.py:253
  1371.4 3.6 add_add_fusion.3
  1375.1 3.0 reduce-scatter.25.cloned.1.call-done
  1378.1 55.0 %reduce-scatter.23.cloned.1.call-done = f32[256,512]{1,0:T(8,128)} async-done(((f32[2048,512]{1,0:T(8,128)}), f32[256,512]{1,0:T(8,128)}) %reduce-scatter.23.cloned.1.call-update) | async-done | bytes 524304 | tf_op jit(solution)/shard_map/reduce_scatter | solution.py:297
  1433.1 55.0 %reduce-scatter.21.cloned.1.call-done = f32[256,512]{1,0:T(8,128)} async-done(((f32[2048,512]{1,0:T(8,128)}), f32[256,512]{1,0:T(8,128)}) %reduce-scatter.21.cloned.1.call-update) | async-done | bytes 524304 | tf_op jit(solution)/shard_map/reduce_scatter | solution.py:296
  1488.0 55.1 %reduce-scatter.19.cloned.1.call-done = f32[256,512]{1,0:T(8,128)} async-done(((f32[2048,512]{1,0:T(8,128)}), f32[256,512]{1,0:T(8,128)}) %reduce-scatter.19.cloned.1.call-update) | async-done | bytes 524304 | tf_op jit(solution)/shard_map/reduce_scatter | solution.py:295
  (310 shorter events, 89.1 us)
Async XLA Ops:
  7.2 9.8 copy-start.61
  7.2 12.0 copy-start.52
  7.2 33.3 %all-gather.14.cloned.1.call-start = ((), (), s32[]{:S(2)}) async-start(), calls=%async_computation.12 | async-start | bytes 2359296 | tf_op jit(solution)/shard_map/all_gather | solution.py:214
  7.9 115.5 %all-gather.10.cloned.1.call-start = ((), (), s32[]{:S(2)}) async-start(), calls=%async_computation.10 | async-start | bytes 5242880 | tf_op jit(solution)/shard_map/all_gather | solution.py:224
  14.9 136.7 %all-gather.16.cloned.1.call-start = ((), (), s32[]{:S(2)}) async-start(), calls=%async_computation.13 | async-start | bytes 2359296 | tf_op jit(solution)/shard_map/all_gather | solution.py:215
  15.7 165.5 %all-gather.12.cloned.1.call-start = ((), (), s32[]{:S(2)}) async-start(), calls=%async_computation.11 | async-start | bytes 2359296 | tf_op jit(solution)/shard_map/all_gather | solution.py:213
  16.3 209.0 %all-gather.18.cloned.1.call-start = ((), (), s32[]{:S(2)}) async-start(), calls=%async_computation.14 | async-start | bytes 2359296 | tf_op jit(solution)/shard_map/all_gather | solution.py:216
  16.9 360.9 %reduce-scatter.11.cloned.1.call-start = ((), (), s32[]{:S(2)}) async-start(), calls=%async_computation.15 | async-start | bytes 10485760 | tf_op jit(solution)/shard_map/reduce_scatter | solution.py:237
  19.3 132.3 %copy-start.59 = (f32[512]{0:T(512)S(1)}, f32[512]{0:T(512)}, u32[]{:S(2)}) copy-start(f32[512]{0:T(512)} %param.33) | copy-start | bytes 6148
  128.7 52.5 %copy-start.60 = (f32[512]{0:T(512)S(1)}, f32[512]{0:T(512)}, u32[]{:S(2)}) copy-start(f32[512]{0:T(512)} %param.30) | copy-start | bytes 6148
  221.9 11.0 copy-start.1
  221.9 11.2 copy-start.5
  225.3 7.7 copy-start.23
  232.9 144.8 %copy-start.7 = (bf16[256,2048]{1,0:T(8,128)(2,1)S(1)}, bf16[256,2048]{1,0:T(8,128)(2,1)}, u32[]{:S(2)}) copy-start(bf16[256,2048]{1,0:T(8,128)(2,1)} %param.26) | copy-start | bytes 3145732
  232.9 144.8 %copy-start.48 = (f32[2048]{0:T(1024)S(1)}, f32[2048]{0:T(1024)}, u32[]{:S(2)}) copy-start(f32[2048]{0:T(1024)} %param.35) | copy-start | bytes 24580
  233.0 147.1 %copy-start.35 = (f32[2048]{0:T(1024)S(1)}, f32[2048]{0:T(1024)}, u32[]{:S(2)}) copy-start(f32[2048]{0:T(1024)} %param.36) | copy-start | bytes 24580
  233.0 147.1 %copy-start.49 = (f32[2048]{0:T(1024)S(1)}, f32[2048]{0:T(1024)}, u32[]{:S(2)}) copy-start(f32[2048]{0:T(1024)} %param.37) | copy-start | bytes 24580
  233.0 265.5 %all-gather.20.cloned.1.call-start = ((), (), s32[]{:S(2)}) async-start(), calls=%async_computation.16 | async-start | bytes 5242880 | tf_op jit(solution)/shard_map/all_gather | solution.py:242
  381.6 136.5 %all-gather.22.cloned.1.call-start = ((), (), s32[]{:S(2)}) async-start(), calls=%async_computation.17 | async-start | bytes 9437184 | tf_op jit(solution)/shard_map/all_gather | solution.py:220
  382.3 296.3 %reduce-scatter.13.cloned.1.call-start = ((), (), s32[]{:S(2)}) async-start(), calls=%async_computation.18 | async-start | bytes 10485760 | tf_op jit(solution)/shard_map/reduce_scatter | solution.py:247
  382.4 15.2 collective-permute-start
  397.5 25.5 %copy-start.25 = (bf16[256,2048]{1,0:T(8,128)(2,1)}, bf16[256,2048]{1,0:T(8,128)(2,1)S(1)}, u32[]{:S(2)}) copy-start(bf16[256,2048]{1,0:T(8,128)(2,1)S(1)} %collective-permute-done) | copy-start | bytes 3145732
  397.5 25.5 %collective-permute-start.1 = (bf16[256,2048]{1,0:T(8,128)(2,1)S(1)}, bf16[256,2048]{1,0:T(8,128)(2,1)S(1)}, u32[]{:S(2)}, u32[]{:S(2)}) collective-permute-start(bf16[256,2048]{1,0:T(8,128)(2,1)S(1)} %collective-permute-done), channel_id=1, source_target_pairs={{0,4},{4,8},{8,12},{12,16},{16,20},{20,24},{24,28},{28,0},{1,5},{5... | collective-permute-start | bytes 3145736 | tf_op jit(solution)/shard_map/ppermute | solution.py:30
  397.6 25.5 %collective-permute-start.4 = (bf16[256,2048]{1,0:T(8,128)(2,1)S(1)}, bf16[256,2048]{1,0:T(8,128)(2,1)}, u32[]{:S(2)}, u32[]{:S(2)}) collective-permute-start(bf16[256,2048]{1,0:T(8,128)(2,1)S(1)} %copy-done.22), channel_id=1, source_target_pairs={{4,0},{8,4},{12,8},{16,12},{20,16},{24,20},{28,24},{0,28},{5,1},{9... | collective-permute-start | bytes 3145736 | tf_op jit(solution)/shard_map/ppermute | solution.py:32
  423.0 25.9 %collective-permute-start.2 = (bf16[256,2048]{1,0:T(8,128)(2,1)S(1)}, bf16[256,2048]{1,0:T(8,128)(2,1)}, u32[]{:S(2)}, u32[]{:S(2)}) collective-permute-start(bf16[256,2048]{1,0:T(8,128)(2,1)S(1)} %collective-permute-done.1), channel_id=1, source_target_pairs={{0,4},{4,8},{8,12},{12,16},{16,20},{20,24},{24,28},{28,0},{1,5},{5... | collective-permute-start | bytes 3145736 | tf_op jit(solution)/shard_map/ppermute | solution.py:30
  423.1 25.9 %collective-permute-start.5 = (bf16[256,2048]{1,0:T(8,128)(2,1)}, bf16[256,2048]{1,0:T(8,128)(2,1)}, u32[]{:S(2)}, u32[]{:S(2)}) collective-permute-start(bf16[256,2048]{1,0:T(8,128)(2,1)} %collective-permute-done.4), channel_id=1, source_target_pairs={{4,0},{8,4},{12,8},{16,12},{20,16},{24,20},{28,24},{0,28},{5,1},{9... | collective-permute-start | bytes 3145736 | tf_op jit(solution)/shard_map/ppermute | solution.py:32
  448.9 26.9 %collective-permute-start.3 = (bf16[256,2048]{1,0:T(8,128)(2,1)}, bf16[256,2048]{1,0:T(8,128)(2,1)}, u32[]{:S(2)}, u32[]{:S(2)}) collective-permute-start(bf16[256,2048]{1,0:T(8,128)(2,1)} %collective-permute-done.2), channel_id=1, source_target_pairs={{0,4},{4,8},{8,12},{12,16},{16,20},{20,24},{24,28},{28,0},{1,5},{5... | collective-permute-start | bytes 3145736 | tf_op jit(solution)/shard_map/ppermute | solution.py:30
  448.9 31.5 %copy-start.28 = (bf16[256,2048]{1,0:T(8,128)(2,1)S(1)}, bf16[256,2048]{1,0:T(8,128)(2,1)}, u32[]{:S(2)}) copy-start(bf16[256,2048]{1,0:T(8,128)(2,1)} %copy-done.27) | copy-start | bytes 3145732
  448.9 32.6 %copy-start.26 = (bf16[256,2048]{1,0:T(8,128)(2,1)S(1)}, bf16[256,2048]{1,0:T(8,128)(2,1)}, u32[]{:S(2)}) copy-start(bf16[256,2048]{1,0:T(8,128)(2,1)} %copy-done.25) | copy-start | bytes 3145732
  449.0 39.3 %collective-permute-start.6 = (bf16[256,2048]{1,0:T(8,128)(2,1)}, bf16[256,2048]{1,0:T(8,128)(2,1)S(1)}, u32[]{:S(2)}, u32[]{:S(2)}) collective-permute-start(bf16[256,2048]{1,0:T(8,128)(2,1)} %collective-permute-done.5), channel_id=1, source_target_pairs={{4,0},{8,4},{12,8},{16,12},{20,16},{24,20},{28,24},{0,28},{5,1},{9... | collective-permute-start | bytes 3145736 | tf_op jit(solution)/shard_map/ppermute | solution.py:32
  489.4 9.1 copy-start.58
  532.8 145.8 %copy-start.29 = (bf16[256,2048]{1,0:T(8,128)(2,1)S(1)}, bf16[256,2048]{1,0:T(8,128)(2,1)}, u32[]{:S(2)}) copy-start(bf16[256,2048]{1,0:T(8,128)(2,1)} %param.42) | copy-start | bytes 3145732
  532.8 145.8 %copy-start.51 = (f32[2048]{0:T(1024)S(1)}, f32[2048]{0:T(1024)}, u32[]{:S(2)}) copy-start(f32[2048]{0:T(1024)} %param.41) | copy-start | bytes 24580
  532.8 231.5 %all-gather.24.cloned.1.call-start = ((), (), s32[]{:S(2)}) async-start(), calls=%async_computation.19 | async-start | bytes 5242880 | tf_op jit(solution)/shard_map/all_gather | solution.py:260
  682.8 254.0 %reduce-scatter.15.cloned.1.call-start = ((), (), s32[]{:S(2)}) async-start(), calls=%async_computation.20 | async-start | bytes 10485760 | tf_op jit(solution)/shard_map/reduce_scatter | solution.py:275
  793.6 233.6 %all-gather.26.cloned.1.call-start = ((), (), s32[]{:S(2)}) async-start(), calls=%async_computation.21 | async-start | bytes 5242880 | tf_op jit(solution)/shard_map/all_gather | solution.py:281
  945.6 238.3 %reduce-scatter.27.cloned.1.call-start = ((), (), s32[]{:S(2)}) async-start(), calls=%async_computation.27 | async-start | bytes 9437184 | tf_op jit(solution)/shard_map/reduce_scatter | solution.py:268
  959.9 227.0 %reduce-scatter.29.cloned.1.call-start = ((), (), s32[]{:S(2)}) async-start(), calls=%async_computation.28 | async-start | bytes 9437184 | tf_op jit(solution)/shard_map/reduce_scatter | solution.py:271
  974.1 60.3 %copy-start.2 = (bf16[1024,8,64]{0,2,1:T(8,128)(2,1)S(1)}, bf16[1024,8,64]{0,2,1:T(8,128)(2,1)}, u32[]{:S(2)}) copy-start(bf16[1024,8,64]{0,2,1:T(8,128)(2,1)} %copy-done.1) | copy-start | bytes 3145732
  974.1 60.3 %copy-start.31 = (f32[8,128]{1,0:T(8,128)S(1)}, f32[8,128]{1,0:T(8,128)}, u32[]{:S(2)}) copy-start(f32[8,128]{1,0:T(8,128)} %copy-done.30) | copy-start | bytes 12292
  974.1 60.3 %copy-start.33 = (f32[2,8,512]{2,1,0:T(8,128)S(1)}, f32[2,8,512]{2,1,0:T(8,128)}, u32[]{:S(2)}) copy-start(f32[2,8,512]{2,1,0:T(8,128)} %copy-done.32) | copy-start | bytes 98308
  974.1 60.3 %copy-start.37 = (bf16[8,8]{1,0:T(8,128)(2,1)S(1)}, bf16[8,8]{1,0:T(8,128)(2,1)}, u32[]{:S(2)}) copy-start(bf16[8,8]{1,0:T(8,128)(2,1)} %copy-done.36) | copy-start | bytes 388
  974.1 60.3 %copy-start.54 = (s32[1024]{0:T(1024)S(1)}, s32[1024]{0:T(1024)}, u32[]{:S(2)}) copy-start(s32[1024]{0:T(1024)} %copy-done.53) | copy-start | bytes 12292
  974.1 60.3 %copy-start.63 = (s32[2]{0:T(128)S(1)}, s32[2]{0:T(128)}, u32[]{:S(2)}) copy-start(s32[2]{0:T(128)} %copy-done.62) | copy-start | bytes 28
  974.2 348.3 %reduce-scatter.17.cloned.1.call-start = ((), (), s32[]{:S(2)}) async-start(), calls=%async_computation.22 | async-start | bytes 10485760 | tf_op jit(solution)/shard_map/reduce_scatter | solution.py:305
  1039.9 9.8 copy-start.3
  1043.7 6.0 copy-start
  1068.0 12.6 copy-start.13
  1090.5 9.3 copy-start.3
  1121.1 12.8 copy-start.13
  1153.6 224.5 %reduce-scatter.25.cloned.1.call-start = ((), (), s32[]{:S(2)}) async-start(), calls=%async_computation.26 | async-start | bytes 4718592 | tf_op jit(solution)/shard_map/reduce_scatter | solution.py:298
  1161.5 271.6 %reduce-scatter.23.cloned.1.call-start = ((), (), s32[]{:S(2)}) async-start(), calls=%async_computation.25 | async-start | bytes 4718592 | tf_op jit(solution)/shard_map/reduce_scatter | solution.py:297
  1168.4 319.7 %reduce-scatter.21.cloned.1.call-start = ((), (), s32[]{:S(2)}) async-start(), calls=%async_computation.24 | async-start | bytes 4718592 | tf_op jit(solution)/shard_map/reduce_scatter | solution.py:296
  1176.2 366.9 %reduce-scatter.19.cloned.1.call-start = ((), (), s32[]{:S(2)}) async-start(), calls=%async_computation.23 | async-start | bytes 4718592 | tf_op jit(solution)/shard_map/reduce_scatter | solution.py:295
  1182.8 139.6 %copy-start.8 = (bf16[256,2048]{1,0:T(8,128)(2,1)S(1)}, bf16[256,2048]{1,0:T(8,128)(2,1)}, u32[]{:S(2)}) copy-start(bf16[256,2048]{1,0:T(8,128)(2,1)} %param.26) | copy-start | bytes 3145732
  1182.8 139.6 %copy-start.34 = (f32[2048]{0:T(1024)S(1)}, f32[2048]{0:T(1024)}, u32[]{:S(2)}) copy-start(f32[2048]{0:T(1024)} %param.27) | copy-start | bytes 24580
  1182.8 139.6 %copy-start.39 = (f32[256]{0:T(256)S(1)}, f32[256]{0:T(256)}, u32[]{:S(2)}) copy-start(f32[256]{0:T(256)} %copy-done.38) | copy-start | bytes 3076
  1186.9 137.8 %copy-start.47 = (f32[256]{0:T(256)S(1)}, f32[256]{0:T(256)}, u32[]{:S(2)}) copy-start(f32[256]{0:T(256)} %copy-done.46) | copy-start | bytes 3076
  1186.9 137.8 %copy-start.45 = (f32[256]{0:T(256)S(1)}, f32[256]{0:T(256)}, u32[]{:S(2)}) copy-start(f32[256]{0:T(256)} %copy-done.44) | copy-start | bytes 3076
  1189.7 136.0 %copy-start.40 = (f32[2048]{0:T(1024)S(1)}, f32[2048]{0:T(1024)}, u32[]{:S(2)}) copy-start(f32[2048]{0:T(1024)} %get-tuple-element.454) | copy-start | bytes 24580
  1189.7 136.0 %copy-start.41 = (f32[2048]{0:T(1024)S(1)}, f32[2048]{0:T(1024)}, u32[]{:S(2)}) copy-start(f32[2048]{0:T(1024)} %get-tuple-element.460) | copy-start | bytes 24580
  1189.7 136.0 %copy-start.42 = (f32[2048]{0:T(1024)S(1)}, f32[2048]{0:T(1024)}, u32[]{:S(2)}) copy-start(f32[2048]{0:T(1024)} %get-tuple-element.527) | copy-start | bytes 24580
  1189.7 136.0 %copy-start.43 = (f32[2048]{0:T(1024)S(1)}, f32[2048]{0:T(1024)}, u32[]{:S(2)}) copy-start(f32[2048]{0:T(1024)} %get-tuple-element.547) | copy-start | bytes 24580
  1189.7 181.7 %copy-start.11 = (f32[256,2048]{1,0:T(8,128)S(1)}, f32[256,2048]{1,0:T(8,128)}, u32[]{:S(2)}) copy-start(f32[256,2048]{1,0:T(8,128)} %copy-done.10) | copy-start | bytes 6291460
  (35 other events, 84.2 us)
Sparse Core Ops, SparseCore 0:
  9.9 30.5 all-gather.13
  42.7 80.7 all-gather.9
  125.3 26.2 all-gather.15
  153.4 27.7 all-gather.11
  182.9 27.7 all-gather.17
  233.1 144.6 reduce-scatter.10
  381.7 81.3 all-gather.19
  465.0 53.0 all-gather.21
  532.9 145.6 reduce-scatter.12
  682.9 81.2 all-gather.23
  793.7 143.0 reduce-scatter.14
  945.7 81.3 all-gather.25
  1030.6 69.9 reduce-scatter.26
  1103.9 71.5 reduce-scatter.28
  1177.7 144.6 reduce-scatter.16
  1326.2 51.8 reduce-scatter.24
  1381.9 51.1 reduce-scatter.22
  1436.9 51.1 reduce-scatter.20
  1492.0 51.1 reduce-scatter.18
